TPU v7x, 128 devices: a whole 4x4x4 slice. The times are simulated.
128 devices in a mesh: ctx: 32 (over x_lo, y, z), tp: 4 (over x_hi, core).
Axes of the slice: x: 4 (x_hi: 2, x_lo: 2; x = x_hi * 2 + x_lo), y: 4, z: 4, core: 2. Of those that a mesh axis runs over, the one named last changes fastest.
Arguments:
- query_rows: bfloat16 [16384, 2048], P('ctx', 'tp'), may hold values from -5 to 5
- key_rows: bfloat16 [16384, 1024], P('ctx', 'tp'), may hold values from -5 to 5
- value_rows: bfloat16 [16384, 1024], P('ctx', 'tp'), may hold values from -6 to 6
Outputs:
- attended: bfloat16 [16384, 2048], P(('ctx', 'tp'))
All inputs are finite; a program needn't handle non-finite values.
Results may differ from a plain program's by a relative error of at most 0.009.
Values may be sent and summed in bfloat16 or wider, within the bound.
No kernel may reach another device: no remote copies, remote signals or barrier semaphores. Data moves between devices by JAX's collectives and lax.ppermute only.
A program may use at most 192 MiB of HBM per device.

v0:
```python
import jax
import jax.numpy as jnp
from jax import lax
from jax.sharding import PartitionSpec as P

HEAD_DIM = 128
SCALAR = 168


lowest = -1e30


def swapped(block, axis, distance):
    count = lax.axis_size(axis)
    route = []
    for low in range(count):
        high = low | 1 << distance
        if high != low and high < count:
            route += [(low, high), (high, low)]
    return lax.ppermute(block, axis, route)


def from_behind(value, axis, steps):
    count = lax.axis_size(axis)
    pairs = [(source, (source + steps) % count) for source in range(count)]
    return lax.ppermute(value, axis, pairs)


def empty_state(q_count, kv_heads, group_size):
    running = jnp.full((kv_heads, group_size, q_count), lowest, jnp.float32)
    totals = jnp.zeros((kv_heads, group_size, q_count), jnp.float32)
    weighted = jnp.zeros((kv_heads, group_size, q_count, HEAD_DIM), jnp.float32)
    return (running, totals, weighted)


def attend_half(state_now, q_part, query_pos, k_part, v_part, key_pos):
    q_count = q_part.shape[0]
    k_count = k_part.shape[0]
    kv_heads = k_part.shape[1] // HEAD_DIM
    group_size = q_part.shape[1] // (HEAD_DIM * kv_heads)

    def compute(current):
        running, totals, weighted = current
        q_heads = q_part.reshape(q_count, kv_heads, group_size, HEAD_DIM)
        k_heads = k_part.reshape(k_count, kv_heads, HEAD_DIM)
        v_heads = v_part.reshape(k_count, kv_heads, HEAD_DIM)
        scores = jnp.einsum(
            "qhgd,khd->hgqk", q_heads, k_heads, preferred_element_type=jnp.float32
        ) * SCALAR ** (-0.5)
        causal = key_pos[None, :] <= query_pos[:, None]
        scores = jnp.where(causal, scores, lowest)
        new_best = jnp.maximum(running, jnp.max(scores, axis=-1))
        weights = jnp.where(causal, jnp.exp(scores - new_best[..., None]), 0.0)
        rescale = jnp.exp(running - new_best)
        totals = totals * rescale + jnp.sum(weights, axis=-1)
        weighted = weighted * rescale[..., None] + jnp.einsum(
            "hgqk,khd->hgqd",
            weights.astype(jnp.bfloat16),
            v_heads,
            preferred_element_type=jnp.float32,
        )
        return (new_best, totals, weighted)

    return lax.cond(key_pos[0] > query_pos[-1], lambda current: current, compute, state_now)


def finish(state_now):
    running, totals, weighted = state_now
    mixed = weighted / totals[..., None]
    q_count = mixed.shape[2]
    return mixed.transpose(2, 0, 1, 3).reshape(q_count, -1).astype(jnp.bfloat16)


def mirror_query(payload):
    for bit_num in range(lax.axis_size("ctx").bit_length() - 1):
        payload = swapped(payload, "ctx", bit_num)
    return payload


def mirror_result(payload):
    for bit_num in range(lax.axis_size("ctx").bit_length() - 1):
        payload = swapped(payload, "ctx", bit_num)
    return payload


def on_device(query_rows, key_rows, value_rows):
    tok_rows = query_rows.shape[0]
    half_rows = tok_rows // 2
    cycle_size = lax.axis_size("ctx")
    cycle_index = lax.axis_index("ctx")
    steps_half = jnp.arange(half_rows, dtype=jnp.int32)
    q_first = query_rows[:half_rows]
    q_second = mirror_query(query_rows[half_rows:])
    pos_first = 2 * cycle_index * half_rows + steps_half
    pos_second = (2 * cycle_size - 1 - 2 * cycle_index) * half_rows + steps_half
    kv_heads = key_rows.shape[1] // HEAD_DIM
    group_size = query_rows.shape[1] // (HEAD_DIM * kv_heads)
    states = (
        empty_state(half_rows, kv_heads, group_size),
        empty_state(half_rows, kv_heads, group_size),
    )

    def absorb(current, k_part, v_part, key_pos):
        return (
            attend_half(current[0], q_first, pos_first, k_part, v_part, key_pos),
            attend_half(current[1], q_second, pos_second, k_part, v_part, key_pos),
        )

    block_steps = jnp.arange(tok_rows, dtype=jnp.int32)

    def advance(step_num, carried):
        k_part, v_part, current = carried
        source = (cycle_index - step_num) % cycle_size
        current = absorb(current, k_part, v_part, source * tok_rows + block_steps)
        k_part, v_part = from_behind((k_part, v_part), "ctx", 1)
        return (k_part, v_part, current)

    k_last, v_last, states = lax.fori_loop(
        0, cycle_size - 1, advance, (key_rows, value_rows, states)
    )
    source = (cycle_index - (cycle_size - 1)) % cycle_size
    states = absorb(states, k_last, v_last, source * tok_rows + block_steps)
    out_first = finish(states[0])
    out_second = mirror_result(finish(states[1]))
    combined = jnp.concatenate([out_first, out_second], axis=0)
    return lax.all_to_all(combined, "tp", split_axis=0, concat_axis=1, tiled=True)


def solution(mesh):
    return jax.shard_map(
        on_device,
        mesh=mesh,
        in_specs=(P("ctx", "tp"), P("ctx", "tp"), P("ctx", "tp")),
        out_specs=P(("ctx", "tp"), None),
        check_vma=False,
    )
```

profile of v0, /device:TPU:1, one launch (start us, length us, event | category | flops | bytes accessed | tf_op | source)
XLA Modules:
  0.0 792.8 jit_solution(18202226632269529525)
XLA Ops:
  39.7 655.8 %while.30 = (s32[]{:T(128)}, bf16[512,256]{1,0:T(8,128)(2,1)S(1)}, bf16[512,256]{1,0:T(8,128)(2,1)S(1)}, f32[2,2,256]{2,1,0:T(2,128)S(1)}, f32[2,2,256]{2,1,0:T(...) while((s32[]{:T(128)}, bf16[512,256]{1,0:T(8,128)(2,1)S(1)}, ...), condition=%wide.region_9.10_spmd.clone, body=%wide.region_0.9_spmd.clone.sunk | while | flops 551293440 | bytes 23798536 | solution.py:118
  46.7 9.6 %conditional.10 = (f32[2,2,256]{2,1,0:T(2,128)S(1)}, f32[2,2,256]{2,1,0:T(2,128)}, f32[2,2,256,128]{3,2,1,0:T(8,128)}) conditional(s32[]{:T(128)} %bitcast.67, (s32[512]{0:T(512)S(1)}, s32[256]{0:T(256)}, bf16[512,256]{1,0:T(8,128)(2,1)}, bf16[256,512]{1,0:T(8,128)(2,1)S(1)}, f32[2,2,256]{2,1,0:T(2,128)S(1)}, /*index=5*/f32[2,2,256]{2,1,0:T(2,128)}, ...), branch_computations={%region_1.3_spmd, %region_4.4_spmd} | conditional | flops 275646464 | bytes 10316880 | solution.py:64
  58.9 9.0 %conditional.11 = (f32[2,2,256]{2,1,0:T(2,128)S(1)}, f32[2,2,256]{2,1,0:T(2,128)}, f32[2,2,256,128]{3,2,1,0:T(8,128)}) conditional(s32[]{:T(128)} %bitcast.68, (s32[512]{0:T(512)S(1)}, s32[256]{0:T(256)}, bf16[512,256]{1,0:T(8,128)(2,1)}, bf16[256,512]{1,0:T(8,128)(2,1)S(1)}, f32[2,2,256]{2,1,0:T(2,128)S(1)}, /*index=5*/f32[2,2,256]{2,1,0:T(2,128)}, ...), branch_computations={%region_5.7_spmd, %region_8.8_spmd} | conditional | flops 275646464 | bytes 10316880 | solution.py:64
  86.3 9.5 %collective-permute-start = (bf16[512,256]{1,0:T(8,128)(2,1)}, bf16[512,256]{1,0:T(8,128)(2,1)S(1)}, u32[]{:S(2)}, u32[]{:S(2)}) collective-permute-start(bf16[512,256]{1,0:T(8,128)(2,1)} %copy.154), channel_id=1, source_target_pairs={{0,4},{4,8},{8,12},{12,16},{16,20},{20,24},{24,28},{28,32},{32,36}... | collective-permute-start | bytes 786440 | tf_op jit(solution)/shard_map/while/body/eval_jaxpr/ppermute | solution.py:26
  114.1 12.1 %collective-permute-start.1 = (bf16[512,256]{1,0:T(8,128)(2,1)}, bf16[512,256]{1,0:T(8,128)(2,1)S(1)}, u32[]{:S(2)}, u32[]{:S(2)}) collective-permute-start(bf16[512,256]{1,0:T(8,128)(2,1)} %copy.155), channel_id=1, source_target_pairs={{0,4},{4,8},{8,12},{12,16},{16,20},{20,24},{24,28},{28,32},{32,36}... | collective-permute-start | bytes 786440 | tf_op jit(solution)/shard_map/while/body/eval_jaxpr/ppermute | solution.py:26
  132.0 9.0 %conditional.11 = (f32[2,2,256]{2,1,0:T(2,128)S(1)}, f32[2,2,256]{2,1,0:T(2,128)}, f32[2,2,256,128]{3,2,1,0:T(8,128)}) conditional(s32[]{:T(128)} %bitcast.68, (s32[512]{0:T(512)S(1)}, s32[256]{0:T(256)}, bf16[512,256]{1,0:T(8,128)(2,1)}, bf16[256,512]{1,0:T(8,128)(2,1)S(1)}, f32[2,2,256]{2,1,0:T(2,128)S(1)}, /*index=5*/f32[2,2,256]{2,1,0:T(2,128)}, ...), branch_computations={%region_5.7_spmd, %region_8.8_spmd} | conditional | flops 275646464 | bytes 10316880 | solution.py:64
  148.6 9.0 %conditional.11 = (f32[2,2,256]{2,1,0:T(2,128)S(1)}, f32[2,2,256]{2,1,0:T(2,128)}, f32[2,2,256,128]{3,2,1,0:T(8,128)}) conditional(s32[]{:T(128)} %bitcast.68, (s32[512]{0:T(512)S(1)}, s32[256]{0:T(256)}, bf16[512,256]{1,0:T(8,128)(2,1)}, bf16[256,512]{1,0:T(8,128)(2,1)S(1)}, f32[2,2,256]{2,1,0:T(2,128)S(1)}, /*index=5*/f32[2,2,256]{2,1,0:T(2,128)}, ...), branch_computations={%region_5.7_spmd, %region_8.8_spmd} | conditional | flops 275646464 | bytes 10316880 | solution.py:64
  158.3 12.5 %collective-permute-start = (bf16[512,256]{1,0:T(8,128)(2,1)}, bf16[512,256]{1,0:T(8,128)(2,1)S(1)}, u32[]{:S(2)}, u32[]{:S(2)}) collective-permute-start(bf16[512,256]{1,0:T(8,128)(2,1)} %copy.154), channel_id=1, source_target_pairs={{0,4},{4,8},{8,12},{12,16},{16,20},{20,24},{24,28},{28,32},{32,36}... | collective-permute-start | bytes 786440 | tf_op jit(solution)/shard_map/while/body/eval_jaxpr/ppermute | solution.py:26
  177.4 9.0 %conditional.11 = (f32[2,2,256]{2,1,0:T(2,128)S(1)}, f32[2,2,256]{2,1,0:T(2,128)}, f32[2,2,256,128]{3,2,1,0:T(8,128)}) conditional(s32[]{:T(128)} %bitcast.68, (s32[512]{0:T(512)S(1)}, s32[256]{0:T(256)}, bf16[512,256]{1,0:T(8,128)(2,1)}, bf16[256,512]{1,0:T(8,128)(2,1)S(1)}, f32[2,2,256]{2,1,0:T(2,128)S(1)}, /*index=5*/f32[2,2,256]{2,1,0:T(2,128)}, ...), branch_computations={%region_5.7_spmd, %region_8.8_spmd} | conditional | flops 275646464 | bytes 10316880 | solution.py:64
  187.8 12.7 %collective-permute-start.1 = (bf16[512,256]{1,0:T(8,128)(2,1)}, bf16[512,256]{1,0:T(8,128)(2,1)S(1)}, u32[]{:S(2)}, u32[]{:S(2)}) collective-permute-start(bf16[512,256]{1,0:T(8,128)(2,1)} %copy.155), channel_id=1, source_target_pairs={{0,4},{4,8},{8,12},{12,16},{16,20},{20,24},{24,28},{28,32},{32,36}... | collective-permute-start | bytes 786440 | tf_op jit(solution)/shard_map/while/body/eval_jaxpr/ppermute | solution.py:26
  222.6 9.0 %conditional.11 = (f32[2,2,256]{2,1,0:T(2,128)S(1)}, f32[2,2,256]{2,1,0:T(2,128)}, f32[2,2,256,128]{3,2,1,0:T(8,128)}) conditional(s32[]{:T(128)} %bitcast.68, (s32[512]{0:T(512)S(1)}, s32[256]{0:T(256)}, bf16[512,256]{1,0:T(8,128)(2,1)}, bf16[256,512]{1,0:T(8,128)(2,1)S(1)}, f32[2,2,256]{2,1,0:T(2,128)S(1)}, /*index=5*/f32[2,2,256]{2,1,0:T(2,128)}, ...), branch_computations={%region_5.7_spmd, %region_8.8_spmd} | conditional | flops 275646464 | bytes 10316880 | solution.py:64
  245.2 9.0 %conditional.11 = (f32[2,2,256]{2,1,0:T(2,128)S(1)}, f32[2,2,256]{2,1,0:T(2,128)}, f32[2,2,256,128]{3,2,1,0:T(8,128)}) conditional(s32[]{:T(128)} %bitcast.68, (s32[512]{0:T(512)S(1)}, s32[256]{0:T(256)}, bf16[512,256]{1,0:T(8,128)(2,1)}, bf16[256,512]{1,0:T(8,128)(2,1)S(1)}, f32[2,2,256]{2,1,0:T(2,128)S(1)}, /*index=5*/f32[2,2,256]{2,1,0:T(2,128)}, ...), branch_computations={%region_5.7_spmd, %region_8.8_spmd} | conditional | flops 275646464 | bytes 10316880 | solution.py:64
  269.3 9.0 %conditional.11 = (f32[2,2,256]{2,1,0:T(2,128)S(1)}, f32[2,2,256]{2,1,0:T(2,128)}, f32[2,2,256,128]{3,2,1,0:T(8,128)}) conditional(s32[]{:T(128)} %bitcast.68, (s32[512]{0:T(512)S(1)}, s32[256]{0:T(256)}, bf16[512,256]{1,0:T(8,128)(2,1)}, bf16[256,512]{1,0:T(8,128)(2,1)S(1)}, f32[2,2,256]{2,1,0:T(2,128)S(1)}, /*index=5*/f32[2,2,256]{2,1,0:T(2,128)}, ...), branch_computations={%region_5.7_spmd, %region_8.8_spmd} | conditional | flops 275646464 | bytes 10316880 | solution.py:64
  285.6 9.0 %conditional.11 = (f32[2,2,256]{2,1,0:T(2,128)S(1)}, f32[2,2,256]{2,1,0:T(2,128)}, f32[2,2,256,128]{3,2,1,0:T(8,128)}) conditional(s32[]{:T(128)} %bitcast.68, (s32[512]{0:T(512)S(1)}, s32[256]{0:T(256)}, bf16[512,256]{1,0:T(8,128)(2,1)}, bf16[256,512]{1,0:T(8,128)(2,1)S(1)}, f32[2,2,256]{2,1,0:T(2,128)S(1)}, /*index=5*/f32[2,2,256]{2,1,0:T(2,128)}, ...), branch_computations={%region_5.7_spmd, %region_8.8_spmd} | conditional | flops 275646464 | bytes 10316880 | solution.py:64
  295.3 9.5 %collective-permute-start = (bf16[512,256]{1,0:T(8,128)(2,1)}, bf16[512,256]{1,0:T(8,128)(2,1)S(1)}, u32[]{:S(2)}, u32[]{:S(2)}) collective-permute-start(bf16[512,256]{1,0:T(8,128)(2,1)} %copy.154), channel_id=1, source_target_pairs={{0,4},{4,8},{8,12},{12,16},{16,20},{20,24},{24,28},{28,32},{32,36}... | collective-permute-start | bytes 786440 | tf_op jit(solution)/shard_map/while/body/eval_jaxpr/ppermute | solution.py:26
  311.4 9.0 %conditional.11 = (f32[2,2,256]{2,1,0:T(2,128)S(1)}, f32[2,2,256]{2,1,0:T(2,128)}, f32[2,2,256,128]{3,2,1,0:T(8,128)}) conditional(s32[]{:T(128)} %bitcast.68, (s32[512]{0:T(512)S(1)}, s32[256]{0:T(256)}, bf16[512,256]{1,0:T(8,128)(2,1)}, bf16[256,512]{1,0:T(8,128)(2,1)S(1)}, f32[2,2,256]{2,1,0:T(2,128)S(1)}, /*index=5*/f32[2,2,256]{2,1,0:T(2,128)}, ...), branch_computations={%region_5.7_spmd, %region_8.8_spmd} | conditional | flops 275646464 | bytes 10316880 | solution.py:64
  321.8 9.5 %collective-permute-start.1 = (bf16[512,256]{1,0:T(8,128)(2,1)}, bf16[512,256]{1,0:T(8,128)(2,1)S(1)}, u32[]{:S(2)}, u32[]{:S(2)}) collective-permute-start(bf16[512,256]{1,0:T(8,128)(2,1)} %copy.155), channel_id=1, source_target_pairs={{0,4},{4,8},{8,12},{12,16},{16,20},{20,24},{24,28},{28,32},{32,36}... | collective-permute-start | bytes 786440 | tf_op jit(solution)/shard_map/while/body/eval_jaxpr/ppermute | solution.py:26
  363.1 9.5 %collective-permute-start = (bf16[512,256]{1,0:T(8,128)(2,1)}, bf16[512,256]{1,0:T(8,128)(2,1)S(1)}, u32[]{:S(2)}, u32[]{:S(2)}) collective-permute-start(bf16[512,256]{1,0:T(8,128)(2,1)} %copy.154), channel_id=1, source_target_pairs={{0,4},{4,8},{8,12},{12,16},{16,20},{20,24},{24,28},{28,32},{32,36}... | collective-permute-start | bytes 786440 | tf_op jit(solution)/shard_map/while/body/eval_jaxpr/ppermute | solution.py:26
  379.2 9.0 %conditional.11 = (f32[2,2,256]{2,1,0:T(2,128)S(1)}, f32[2,2,256]{2,1,0:T(2,128)}, f32[2,2,256,128]{3,2,1,0:T(8,128)}) conditional(s32[]{:T(128)} %bitcast.68, (s32[512]{0:T(512)S(1)}, s32[256]{0:T(256)}, bf16[512,256]{1,0:T(8,128)(2,1)}, bf16[256,512]{1,0:T(8,128)(2,1)S(1)}, f32[2,2,256]{2,1,0:T(2,128)S(1)}, /*index=5*/f32[2,2,256]{2,1,0:T(2,128)}, ...), branch_computations={%region_5.7_spmd, %region_8.8_spmd} | conditional | flops 275646464 | bytes 10316880 | solution.py:64
  396.0 9.0 %conditional.11 = (f32[2,2,256]{2,1,0:T(2,128)S(1)}, f32[2,2,256]{2,1,0:T(2,128)}, f32[2,2,256,128]{3,2,1,0:T(8,128)}) conditional(s32[]{:T(128)} %bitcast.68, (s32[512]{0:T(512)S(1)}, s32[256]{0:T(256)}, bf16[512,256]{1,0:T(8,128)(2,1)}, bf16[256,512]{1,0:T(8,128)(2,1)S(1)}, f32[2,2,256]{2,1,0:T(2,128)S(1)}, /*index=5*/f32[2,2,256]{2,1,0:T(2,128)}, ...), branch_computations={%region_5.7_spmd, %region_8.8_spmd} | conditional | flops 275646464 | bytes 10316880 | solution.py:64
  480.1 9.0 %conditional.11 = (f32[2,2,256]{2,1,0:T(2,128)S(1)}, f32[2,2,256]{2,1,0:T(2,128)}, f32[2,2,256,128]{3,2,1,0:T(8,128)}) conditional(s32[]{:T(128)} %bitcast.68, (s32[512]{0:T(512)S(1)}, s32[256]{0:T(256)}, bf16[512,256]{1,0:T(8,128)(2,1)}, bf16[256,512]{1,0:T(8,128)(2,1)S(1)}, f32[2,2,256]{2,1,0:T(2,128)S(1)}, /*index=5*/f32[2,2,256]{2,1,0:T(2,128)}, ...), branch_computations={%region_5.7_spmd, %region_8.8_spmd} | conditional | flops 275646464 | bytes 10316880 | solution.py:64
  489.9 9.5 %collective-permute-start = (bf16[512,256]{1,0:T(8,128)(2,1)}, bf16[512,256]{1,0:T(8,128)(2,1)S(1)}, u32[]{:S(2)}, u32[]{:S(2)}) collective-permute-start(bf16[512,256]{1,0:T(8,128)(2,1)} %copy.154), channel_id=1, source_target_pairs={{0,4},{4,8},{8,12},{12,16},{16,20},{20,24},{24,28},{28,32},{32,36}... | collective-permute-start | bytes 786440 | tf_op jit(solution)/shard_map/while/body/eval_jaxpr/ppermute | solution.py:26
  505.9 9.0 %conditional.11 = (f32[2,2,256]{2,1,0:T(2,128)S(1)}, f32[2,2,256]{2,1,0:T(2,128)}, f32[2,2,256,128]{3,2,1,0:T(8,128)}) conditional(s32[]{:T(128)} %bitcast.68, (s32[512]{0:T(512)S(1)}, s32[256]{0:T(256)}, bf16[512,256]{1,0:T(8,128)(2,1)}, bf16[256,512]{1,0:T(8,128)(2,1)S(1)}, f32[2,2,256]{2,1,0:T(2,128)S(1)}, /*index=5*/f32[2,2,256]{2,1,0:T(2,128)}, ...), branch_computations={%region_5.7_spmd, %region_8.8_spmd} | conditional | flops 275646464 | bytes 10316880 | solution.py:64
  516.4 9.5 %collective-permute-start.1 = (bf16[512,256]{1,0:T(8,128)(2,1)}, bf16[512,256]{1,0:T(8,128)(2,1)S(1)}, u32[]{:S(2)}, u32[]{:S(2)}) collective-permute-start(bf16[512,256]{1,0:T(8,128)(2,1)} %copy.155), channel_id=1, source_target_pairs={{0,4},{4,8},{8,12},{12,16},{16,20},{20,24},{24,28},{28,32},{32,36}... | collective-permute-start | bytes 786440 | tf_op jit(solution)/shard_map/while/body/eval_jaxpr/ppermute | solution.py:26
  548.0 9.0 %conditional.11 = (f32[2,2,256]{2,1,0:T(2,128)S(1)}, f32[2,2,256]{2,1,0:T(2,128)}, f32[2,2,256,128]{3,2,1,0:T(8,128)}) conditional(s32[]{:T(128)} %bitcast.68, (s32[512]{0:T(512)S(1)}, s32[256]{0:T(256)}, bf16[512,256]{1,0:T(8,128)(2,1)}, bf16[256,512]{1,0:T(8,128)(2,1)S(1)}, f32[2,2,256]{2,1,0:T(2,128)S(1)}, /*index=5*/f32[2,2,256]{2,1,0:T(2,128)}, ...), branch_computations={%region_5.7_spmd, %region_8.8_spmd} | conditional | flops 275646464 | bytes 10316880 | solution.py:64
  566.5 9.0 %conditional.11 = (f32[2,2,256]{2,1,0:T(2,128)S(1)}, f32[2,2,256]{2,1,0:T(2,128)}, f32[2,2,256,128]{3,2,1,0:T(8,128)}) conditional(s32[]{:T(128)} %bitcast.68, (s32[512]{0:T(512)S(1)}, s32[256]{0:T(256)}, bf16[512,256]{1,0:T(8,128)(2,1)}, bf16[256,512]{1,0:T(8,128)(2,1)S(1)}, f32[2,2,256]{2,1,0:T(2,128)S(1)}, /*index=5*/f32[2,2,256]{2,1,0:T(2,128)}, ...), branch_computations={%region_5.7_spmd, %region_8.8_spmd} | conditional | flops 275646464 | bytes 10316880 | solution.py:64
  584.6 9.0 %conditional.11 = (f32[2,2,256]{2,1,0:T(2,128)S(1)}, f32[2,2,256]{2,1,0:T(2,128)}, f32[2,2,256,128]{3,2,1,0:T(8,128)}) conditional(s32[]{:T(128)} %bitcast.68, (s32[512]{0:T(512)S(1)}, s32[256]{0:T(256)}, bf16[512,256]{1,0:T(8,128)(2,1)}, bf16[256,512]{1,0:T(8,128)(2,1)S(1)}, f32[2,2,256]{2,1,0:T(2,128)S(1)}, /*index=5*/f32[2,2,256]{2,1,0:T(2,128)}, ...), branch_computations={%region_5.7_spmd, %region_8.8_spmd} | conditional | flops 275646464 | bytes 10316880 | solution.py:64
  602.3 9.0 %conditional.11 = (f32[2,2,256]{2,1,0:T(2,128)S(1)}, f32[2,2,256]{2,1,0:T(2,128)}, f32[2,2,256,128]{3,2,1,0:T(8,128)}) conditional(s32[]{:T(128)} %bitcast.68, (s32[512]{0:T(512)S(1)}, s32[256]{0:T(256)}, bf16[512,256]{1,0:T(8,128)(2,1)}, bf16[256,512]{1,0:T(8,128)(2,1)S(1)}, f32[2,2,256]{2,1,0:T(2,128)S(1)}, /*index=5*/f32[2,2,256]{2,1,0:T(2,128)}, ...), branch_computations={%region_5.7_spmd, %region_8.8_spmd} | conditional | flops 275646464 | bytes 10316880 | solution.py:64
  619.9 9.0 %conditional.11 = (f32[2,2,256]{2,1,0:T(2,128)S(1)}, f32[2,2,256]{2,1,0:T(2,128)}, f32[2,2,256,128]{3,2,1,0:T(8,128)}) conditional(s32[]{:T(128)} %bitcast.68, (s32[512]{0:T(512)S(1)}, s32[256]{0:T(256)}, bf16[512,256]{1,0:T(8,128)(2,1)}, bf16[256,512]{1,0:T(8,128)(2,1)S(1)}, f32[2,2,256]{2,1,0:T(2,128)S(1)}, /*index=5*/f32[2,2,256]{2,1,0:T(2,128)}, ...), branch_computations={%region_5.7_spmd, %region_8.8_spmd} | conditional | flops 275646464 | bytes 10316880 | solution.py:64
  686.4 9.0 %conditional.11 = (f32[2,2,256]{2,1,0:T(2,128)S(1)}, f32[2,2,256]{2,1,0:T(2,128)}, f32[2,2,256,128]{3,2,1,0:T(8,128)}) conditional(s32[]{:T(128)} %bitcast.68, (s32[512]{0:T(512)S(1)}, s32[256]{0:T(256)}, bf16[512,256]{1,0:T(8,128)(2,1)}, bf16[256,512]{1,0:T(8,128)(2,1)S(1)}, f32[2,2,256]{2,1,0:T(2,128)S(1)}, /*index=5*/f32[2,2,256]{2,1,0:T(2,128)}, ...), branch_computations={%region_5.7_spmd, %region_8.8_spmd} | conditional | flops 275646464 | bytes 10316880 | solution.py:64
  742.7 11.4 %collective-permute-start.11 = (bf16[256,512]{0,1:T(8,128)(2,1)}, bf16[256,512]{0,1:T(8,128)(2,1)}, u32[]{:S(2)}, u32[]{:S(2)}) collective-permute-start(bf16[256,512]{0,1:T(8,128)(2,1)} %collective-permute-done.10), channel_id=1, source_target_pairs={{0,64},{64,0},{4,68},{68,4},{8,72},{72,8},{12,76},{76,12},{16,80},... | collective-permute-start | bytes 786440 | tf_op jit(solution)/shard_map/ppermute | solution.py:20
  759.4 32.1 %all_to_all.19 = bf16[4,128,512]{2,1,0:T(8,128)(2,1)S(1)} all-to-all(bf16[4,128,512]{2,1,0:T(8,128)(2,1)S(1)} %bitcast.73), channel_id=1, replica_groups=mesh['ctx'=32,'tp'=4] {'tp'}, dimensions={0} | all-to-all | bytes 1048576 | tf_op jit(solution)/shard_map/all_to_all | solution.py:126
  (917 shorter events, 688.6 us)
Async XLA Ops:
  40.4 27.5 %collective-permute-start = (bf16[512,256]{1,0:T(8,128)(2,1)}, bf16[512,256]{1,0:T(8,128)(2,1)S(1)}, u32[]{:S(2)}, u32[]{:S(2)}) collective-permute-start(bf16[512,256]{1,0:T(8,128)(2,1)} %copy.154), channel_id=1, source_target_pairs={{0,4},{4,8},{8,12},{12,16},{16,20},{20,24},{24,28},{28,32},{32,36}... | collective-permute-start | bytes 786440 | tf_op jit(solution)/shard_map/while/body/eval_jaxpr/ppermute | solution.py:26
  42.0 26.0 %collective-permute-start.1 = (bf16[512,256]{1,0:T(8,128)(2,1)}, bf16[512,256]{1,0:T(8,128)(2,1)S(1)}, u32[]{:S(2)}, u32[]{:S(2)}) collective-permute-start(bf16[512,256]{1,0:T(8,128)(2,1)} %copy.155), channel_id=1, source_target_pairs={{0,4},{4,8},{8,12},{12,16},{16,20},{20,24},{24,28},{28,32},{32,36}... | collective-permute-start | bytes 786440 | tf_op jit(solution)/shard_map/while/body/eval_jaxpr/ppermute | solution.py:26
  68.7 16.9 %collective-permute-start = (bf16[512,256]{1,0:T(8,128)(2,1)}, bf16[512,256]{1,0:T(8,128)(2,1)S(1)}, u32[]{:S(2)}, u32[]{:S(2)}) collective-permute-start(bf16[512,256]{1,0:T(8,128)(2,1)} %copy.154), channel_id=1, source_target_pairs={{0,4},{4,8},{8,12},{12,16},{16,20},{20,24},{24,28},{28,32},{32,36}... | collective-permute-start | bytes 786440 | tf_op jit(solution)/shard_map/while/body/eval_jaxpr/ppermute | solution.py:26
  86.3 26.4 %collective-permute-start = (bf16[512,256]{1,0:T(8,128)(2,1)}, bf16[512,256]{1,0:T(8,128)(2,1)S(1)}, u32[]{:S(2)}, u32[]{:S(2)}) collective-permute-start(bf16[512,256]{1,0:T(8,128)(2,1)} %copy.154), channel_id=1, source_target_pairs={{0,4},{4,8},{8,12},{12,16},{16,20},{20,24},{24,28},{28,32},{32,36}... | collective-permute-start | bytes 786440 | tf_op jit(solution)/shard_map/while/body/eval_jaxpr/ppermute | solution.py:26
  113.4 27.6 %collective-permute-start = (bf16[512,256]{1,0:T(8,128)(2,1)}, bf16[512,256]{1,0:T(8,128)(2,1)S(1)}, u32[]{:S(2)}, u32[]{:S(2)}) collective-permute-start(bf16[512,256]{1,0:T(8,128)(2,1)} %copy.154), channel_id=1, source_target_pairs={{0,4},{4,8},{8,12},{12,16},{16,20},{20,24},{24,28},{28,32},{32,36}... | collective-permute-start | bytes 786440 | tf_op jit(solution)/shard_map/while/body/eval_jaxpr/ppermute | solution.py:26
  114.1 26.9 %collective-permute-start.1 = (bf16[512,256]{1,0:T(8,128)(2,1)}, bf16[512,256]{1,0:T(8,128)(2,1)S(1)}, u32[]{:S(2)}, u32[]{:S(2)}) collective-permute-start(bf16[512,256]{1,0:T(8,128)(2,1)} %copy.155), channel_id=1, source_target_pairs={{0,4},{4,8},{8,12},{12,16},{16,20},{20,24},{24,28},{28,32},{32,36}... | collective-permute-start | bytes 786440 | tf_op jit(solution)/shard_map/while/body/eval_jaxpr/ppermute | solution.py:26
  158.3 28.0 %collective-permute-start = (bf16[512,256]{1,0:T(8,128)(2,1)}, bf16[512,256]{1,0:T(8,128)(2,1)S(1)}, u32[]{:S(2)}, u32[]{:S(2)}) collective-permute-start(bf16[512,256]{1,0:T(8,128)(2,1)} %copy.154), channel_id=1, source_target_pairs={{0,4},{4,8},{8,12},{12,16},{16,20},{20,24},{24,28},{28,32},{32,36}... | collective-permute-start | bytes 786440 | tf_op jit(solution)/shard_map/while/body/eval_jaxpr/ppermute | solution.py:26
  187.1 28.3 %collective-permute-start = (bf16[512,256]{1,0:T(8,128)(2,1)}, bf16[512,256]{1,0:T(8,128)(2,1)S(1)}, u32[]{:S(2)}, u32[]{:S(2)}) collective-permute-start(bf16[512,256]{1,0:T(8,128)(2,1)} %copy.154), channel_id=1, source_target_pairs={{0,4},{4,8},{8,12},{12,16},{16,20},{20,24},{24,28},{28,32},{32,36}... | collective-permute-start | bytes 786440 | tf_op jit(solution)/shard_map/while/body/eval_jaxpr/ppermute | solution.py:26
  187.8 27.5 %collective-permute-start.1 = (bf16[512,256]{1,0:T(8,128)(2,1)}, bf16[512,256]{1,0:T(8,128)(2,1)S(1)}, u32[]{:S(2)}, u32[]{:S(2)}) collective-permute-start(bf16[512,256]{1,0:T(8,128)(2,1)} %copy.155), channel_id=1, source_target_pairs={{0,4},{4,8},{8,12},{12,16},{16,20},{20,24},{24,28},{28,32},{32,36}... | collective-permute-start | bytes 786440 | tf_op jit(solution)/shard_map/while/body/eval_jaxpr/ppermute | solution.py:26
  232.4 21.8 %collective-permute-start = (bf16[512,256]{1,0:T(8,128)(2,1)}, bf16[512,256]{1,0:T(8,128)(2,1)S(1)}, u32[]{:S(2)}, u32[]{:S(2)}) collective-permute-start(bf16[512,256]{1,0:T(8,128)(2,1)} %copy.154), channel_id=1, source_target_pairs={{0,4},{4,8},{8,12},{12,16},{16,20},{20,24},{24,28},{28,32},{32,36}... | collective-permute-start | bytes 786440 | tf_op jit(solution)/shard_map/while/body/eval_jaxpr/ppermute | solution.py:26
  237.7 16.5 %collective-permute-start.1 = (bf16[512,256]{1,0:T(8,128)(2,1)}, bf16[512,256]{1,0:T(8,128)(2,1)S(1)}, u32[]{:S(2)}, u32[]{:S(2)}) collective-permute-start(bf16[512,256]{1,0:T(8,128)(2,1)} %copy.155), channel_id=1, source_target_pairs={{0,4},{4,8},{8,12},{12,16},{16,20},{20,24},{24,28},{28,32},{32,36}... | collective-permute-start | bytes 786440 | tf_op jit(solution)/shard_map/while/body/eval_jaxpr/ppermute | solution.py:26
  254.9 23.4 %collective-permute-start = (bf16[512,256]{1,0:T(8,128)(2,1)}, bf16[512,256]{1,0:T(8,128)(2,1)S(1)}, u32[]{:S(2)}, u32[]{:S(2)}) collective-permute-start(bf16[512,256]{1,0:T(8,128)(2,1)} %copy.154), channel_id=1, source_target_pairs={{0,4},{4,8},{8,12},{12,16},{16,20},{20,24},{24,28},{28,32},{32,36}... | collective-permute-start | bytes 786440 | tf_op jit(solution)/shard_map/while/body/eval_jaxpr/ppermute | solution.py:26
  255.6 22.7 %collective-permute-start.1 = (bf16[512,256]{1,0:T(8,128)(2,1)}, bf16[512,256]{1,0:T(8,128)(2,1)S(1)}, u32[]{:S(2)}, u32[]{:S(2)}) collective-permute-start(bf16[512,256]{1,0:T(8,128)(2,1)} %copy.155), channel_id=1, source_target_pairs={{0,4},{4,8},{8,12},{12,16},{16,20},{20,24},{24,28},{28,32},{32,36}... | collective-permute-start | bytes 786440 | tf_op jit(solution)/shard_map/while/body/eval_jaxpr/ppermute | solution.py:26
  295.3 25.1 %collective-permute-start = (bf16[512,256]{1,0:T(8,128)(2,1)}, bf16[512,256]{1,0:T(8,128)(2,1)S(1)}, u32[]{:S(2)}, u32[]{:S(2)}) collective-permute-start(bf16[512,256]{1,0:T(8,128)(2,1)} %copy.154), channel_id=1, source_target_pairs={{0,4},{4,8},{8,12},{12,16},{16,20},{20,24},{24,28},{28,32},{32,36}... | collective-permute-start | bytes 786440 | tf_op jit(solution)/shard_map/while/body/eval_jaxpr/ppermute | solution.py:26
  321.1 25.1 %collective-permute-start = (bf16[512,256]{1,0:T(8,128)(2,1)}, bf16[512,256]{1,0:T(8,128)(2,1)S(1)}, u32[]{:S(2)}, u32[]{:S(2)}) collective-permute-start(bf16[512,256]{1,0:T(8,128)(2,1)} %copy.154), channel_id=1, source_target_pairs={{0,4},{4,8},{8,12},{12,16},{16,20},{20,24},{24,28},{28,32},{32,36}... | collective-permute-start | bytes 786440 | tf_op jit(solution)/shard_map/while/body/eval_jaxpr/ppermute | solution.py:26
  321.8 24.3 %collective-permute-start.1 = (bf16[512,256]{1,0:T(8,128)(2,1)}, bf16[512,256]{1,0:T(8,128)(2,1)S(1)}, u32[]{:S(2)}, u32[]{:S(2)}) collective-permute-start(bf16[512,256]{1,0:T(8,128)(2,1)} %copy.155), channel_id=1, source_target_pairs={{0,4},{4,8},{8,12},{12,16},{16,20},{20,24},{24,28},{28,32},{32,36}... | collective-permute-start | bytes 786440 | tf_op jit(solution)/shard_map/while/body/eval_jaxpr/ppermute | solution.py:26
  363.1 25.1 %collective-permute-start = (bf16[512,256]{1,0:T(8,128)(2,1)}, bf16[512,256]{1,0:T(8,128)(2,1)S(1)}, u32[]{:S(2)}, u32[]{:S(2)}) collective-permute-start(bf16[512,256]{1,0:T(8,128)(2,1)} %copy.154), channel_id=1, source_target_pairs={{0,4},{4,8},{8,12},{12,16},{16,20},{20,24},{24,28},{28,32},{32,36}... | collective-permute-start | bytes 786440 | tf_op jit(solution)/shard_map/while/body/eval_jaxpr/ppermute | solution.py:26
  405.8 19.3 %collective-permute-start = (bf16[512,256]{1,0:T(8,128)(2,1)}, bf16[512,256]{1,0:T(8,128)(2,1)S(1)}, u32[]{:S(2)}, u32[]{:S(2)}) collective-permute-start(bf16[512,256]{1,0:T(8,128)(2,1)} %copy.154), channel_id=1, source_target_pairs={{0,4},{4,8},{8,12},{12,16},{16,20},{20,24},{24,28},{28,32},{32,36}... | collective-permute-start | bytes 786440 | tf_op jit(solution)/shard_map/while/body/eval_jaxpr/ppermute | solution.py:26
  406.5 18.6 %collective-permute-start.1 = (bf16[512,256]{1,0:T(8,128)(2,1)}, bf16[512,256]{1,0:T(8,128)(2,1)S(1)}, u32[]{:S(2)}, u32[]{:S(2)}) collective-permute-start(bf16[512,256]{1,0:T(8,128)(2,1)} %copy.155), channel_id=1, source_target_pairs={{0,4},{4,8},{8,12},{12,16},{16,20},{20,24},{24,28},{28,32},{32,36}... | collective-permute-start | bytes 786440 | tf_op jit(solution)/shard_map/while/body/eval_jaxpr/ppermute | solution.py:26
  425.8 23.0 %collective-permute-start = (bf16[512,256]{1,0:T(8,128)(2,1)}, bf16[512,256]{1,0:T(8,128)(2,1)S(1)}, u32[]{:S(2)}, u32[]{:S(2)}) collective-permute-start(bf16[512,256]{1,0:T(8,128)(2,1)} %copy.154), channel_id=1, source_target_pairs={{0,4},{4,8},{8,12},{12,16},{16,20},{20,24},{24,28},{28,32},{32,36}... | collective-permute-start | bytes 786440 | tf_op jit(solution)/shard_map/while/body/eval_jaxpr/ppermute | solution.py:26
  432.3 16.5 %collective-permute-start.1 = (bf16[512,256]{1,0:T(8,128)(2,1)}, bf16[512,256]{1,0:T(8,128)(2,1)S(1)}, u32[]{:S(2)}, u32[]{:S(2)}) collective-permute-start(bf16[512,256]{1,0:T(8,128)(2,1)} %copy.155), channel_id=1, source_target_pairs={{0,4},{4,8},{8,12},{12,16},{16,20},{20,24},{24,28},{28,32},{32,36}... | collective-permute-start | bytes 786440 | tf_op jit(solution)/shard_map/while/body/eval_jaxpr/ppermute | solution.py:26
  449.5 23.4 %collective-permute-start = (bf16[512,256]{1,0:T(8,128)(2,1)}, bf16[512,256]{1,0:T(8,128)(2,1)S(1)}, u32[]{:S(2)}, u32[]{:S(2)}) collective-permute-start(bf16[512,256]{1,0:T(8,128)(2,1)} %copy.154), channel_id=1, source_target_pairs={{0,4},{4,8},{8,12},{12,16},{16,20},{20,24},{24,28},{28,32},{32,36}... | collective-permute-start | bytes 786440 | tf_op jit(solution)/shard_map/while/body/eval_jaxpr/ppermute | solution.py:26
  450.2 22.7 %collective-permute-start.1 = (bf16[512,256]{1,0:T(8,128)(2,1)}, bf16[512,256]{1,0:T(8,128)(2,1)S(1)}, u32[]{:S(2)}, u32[]{:S(2)}) collective-permute-start(bf16[512,256]{1,0:T(8,128)(2,1)} %copy.155), channel_id=1, source_target_pairs={{0,4},{4,8},{8,12},{12,16},{16,20},{20,24},{24,28},{28,32},{32,36}... | collective-permute-start | bytes 786440 | tf_op jit(solution)/shard_map/while/body/eval_jaxpr/ppermute | solution.py:26
  489.9 25.1 %collective-permute-start = (bf16[512,256]{1,0:T(8,128)(2,1)}, bf16[512,256]{1,0:T(8,128)(2,1)S(1)}, u32[]{:S(2)}, u32[]{:S(2)}) collective-permute-start(bf16[512,256]{1,0:T(8,128)(2,1)} %copy.154), channel_id=1, source_target_pairs={{0,4},{4,8},{8,12},{12,16},{16,20},{20,24},{24,28},{28,32},{32,36}... | collective-permute-start | bytes 786440 | tf_op jit(solution)/shard_map/while/body/eval_jaxpr/ppermute | solution.py:26
  515.7 25.1 %collective-permute-start = (bf16[512,256]{1,0:T(8,128)(2,1)}, bf16[512,256]{1,0:T(8,128)(2,1)S(1)}, u32[]{:S(2)}, u32[]{:S(2)}) collective-permute-start(bf16[512,256]{1,0:T(8,128)(2,1)} %copy.154), channel_id=1, source_target_pairs={{0,4},{4,8},{8,12},{12,16},{16,20},{20,24},{24,28},{28,32},{32,36}... | collective-permute-start | bytes 786440 | tf_op jit(solution)/shard_map/while/body/eval_jaxpr/ppermute | solution.py:26
  516.4 24.3 %collective-permute-start.1 = (bf16[512,256]{1,0:T(8,128)(2,1)}, bf16[512,256]{1,0:T(8,128)(2,1)S(1)}, u32[]{:S(2)}, u32[]{:S(2)}) collective-permute-start(bf16[512,256]{1,0:T(8,128)(2,1)} %copy.155), channel_id=1, source_target_pairs={{0,4},{4,8},{8,12},{12,16},{16,20},{20,24},{24,28},{28,32},{32,36}... | collective-permute-start | bytes 786440 | tf_op jit(solution)/shard_map/while/body/eval_jaxpr/ppermute | solution.py:26
  557.7 17.8 %collective-permute-start = (bf16[512,256]{1,0:T(8,128)(2,1)}, bf16[512,256]{1,0:T(8,128)(2,1)S(1)}, u32[]{:S(2)}, u32[]{:S(2)}) collective-permute-start(bf16[512,256]{1,0:T(8,128)(2,1)} %copy.154), channel_id=1, source_target_pairs={{0,4},{4,8},{8,12},{12,16},{16,20},{20,24},{24,28},{28,32},{32,36}... | collective-permute-start | bytes 786440 | tf_op jit(solution)/shard_map/while/body/eval_jaxpr/ppermute | solution.py:26
  559.0 16.5 %collective-permute-start.1 = (bf16[512,256]{1,0:T(8,128)(2,1)}, bf16[512,256]{1,0:T(8,128)(2,1)S(1)}, u32[]{:S(2)}, u32[]{:S(2)}) collective-permute-start(bf16[512,256]{1,0:T(8,128)(2,1)} %copy.155), channel_id=1, source_target_pairs={{0,4},{4,8},{8,12},{12,16},{16,20},{20,24},{24,28},{28,32},{32,36}... | collective-permute-start | bytes 786440 | tf_op jit(solution)/shard_map/while/body/eval_jaxpr/ppermute | solution.py:26
  576.2 17.4 %collective-permute-start = (bf16[512,256]{1,0:T(8,128)(2,1)}, bf16[512,256]{1,0:T(8,128)(2,1)S(1)}, u32[]{:S(2)}, u32[]{:S(2)}) collective-permute-start(bf16[512,256]{1,0:T(8,128)(2,1)} %copy.154), channel_id=1, source_target_pairs={{0,4},{4,8},{8,12},{12,16},{16,20},{20,24},{24,28},{28,32},{32,36}... | collective-permute-start | bytes 786440 | tf_op jit(solution)/shard_map/while/body/eval_jaxpr/ppermute | solution.py:26
  594.4 17.0 %collective-permute-start = (bf16[512,256]{1,0:T(8,128)(2,1)}, bf16[512,256]{1,0:T(8,128)(2,1)S(1)}, u32[]{:S(2)}, u32[]{:S(2)}) collective-permute-start(bf16[512,256]{1,0:T(8,128)(2,1)} %copy.154), channel_id=1, source_target_pairs={{0,4},{4,8},{8,12},{12,16},{16,20},{20,24},{24,28},{28,32},{32,36}... | collective-permute-start | bytes 786440 | tf_op jit(solution)/shard_map/while/body/eval_jaxpr/ppermute | solution.py:26
  612.1 16.8 %collective-permute-start = (bf16[512,256]{1,0:T(8,128)(2,1)}, bf16[512,256]{1,0:T(8,128)(2,1)S(1)}, u32[]{:S(2)}, u32[]{:S(2)}) collective-permute-start(bf16[512,256]{1,0:T(8,128)(2,1)} %copy.154), channel_id=1, source_target_pairs={{0,4},{4,8},{8,12},{12,16},{16,20},{20,24},{24,28},{28,32},{32,36}... | collective-permute-start | bytes 786440 | tf_op jit(solution)/shard_map/while/body/eval_jaxpr/ppermute | solution.py:26
  662.2 16.4 %collective-permute-start = (bf16[512,256]{1,0:T(8,128)(2,1)}, bf16[512,256]{1,0:T(8,128)(2,1)S(1)}, u32[]{:S(2)}, u32[]{:S(2)}) collective-permute-start(bf16[512,256]{1,0:T(8,128)(2,1)} %copy.154), channel_id=1, source_target_pairs={{0,4},{4,8},{8,12},{12,16},{16,20},{20,24},{24,28},{28,32},{32,36}... | collective-permute-start | bytes 786440 | tf_op jit(solution)/shard_map/while/body/eval_jaxpr/ppermute | solution.py:26
  (112 other events, 884.3 us)
where the time goes:
time: 800 us; the launch traced here: 793 us
  local copies, waits for them, and re-layouts  246 us (31%)
  starting transfers between devices  187 us (23%)
  matrix products  138 us (17%)
  loops' own time  83.2 us (10%)
  other arithmetic  67.3 us (8%)
  waiting for transfers between devices  36.9 us (5%)
  blocking collectives  32.1 us (4%)
    ppermute x62, starting transfers between devices, from_behind(): return lax.ppermute(value, axis, pairs)  142 us
    dot_general x33, matrix products, compute(): jnp.einsum('hgqk,khd->hgqd', weights.astype(jnp.bfloat16), v_heads, prefe...  90.1 us
    slice x64, local copies, waits for them, and re-layouts, attend_half(): query_pos[-1]  85 us
    another operation x1, loops' own time, on_device(): lax.fori_loop(0, cycle_size - 1, advance, (key_rows, value_rows, states))  80.4 us
    dot_general x33, matrix products, compute(): jnp.einsum('qhgd,khd->hgqk', q_heads, k_heads, preferred_element_type=jnp...  47.7 us
    ppermute x10, starting transfers between devices, swapped(): return lax.ppermute(block, axis, route)  44.4 us
    while x124, local copies, waits for them, and re-layouts  44.1 us
    ppermute x10, waiting for transfers between devices, swapped(): return lax.ppermute(block, axis, route)  36.8 us
  transfers between devices with their start and end apart: 72, of which 10 were waited for; matrix products, arithmetic and copies ran while one was open for 52% of the time, Pallas kernels for 0%

commit v1 on v0

v1 whole, which is shorter than its diff:
```python
import jax
import jax.numpy as jnp
from jax import lax
from jax.experimental import pallas as pl
from jax.experimental.pallas import tpu as pltpu
from jax.sharding import Mesh, PartitionSpec as P

HEAD_DIM = 128
SCALAR = 168
SCALE = SCALAR ** (-0.5) * 1.4426950408889634
LOWEST = -1e30
BLOCK = 512
ROWS = 2 * BLOCK
EXT = HEAD_DIM + 16

CONTRACT_LAST = (((1,), (1,)), ((), ()))
PARAMS = pltpu.CompilerParams(vmem_limit_bytes=52 * 2**20)


def vmem(count):
    return [pl.BlockSpec(memory_space=pltpu.VMEM)] * count


def smem():
    return pl.BlockSpec(memory_space=pltpu.SMEM)


def pack_kernel(place, query_ref, key_ref, value_ref, q_own, q_other, kv_own, kv_other):
    half = place[0]
    for head, q_out, kv_out in ((half, q_own, kv_own), (1 - half, q_other, kv_other)):
        for part in range(2):
            at = pl.multiple_of(head * 256 + part * 128, 128)
            q_out[part * BLOCK : (part + 1) * BLOCK] = query_ref[:, pl.ds(at, 128)]
        at = pl.multiple_of(head * 128, 128)
        kv_out[:BLOCK] = key_ref[:, pl.ds(at, 128)]
        for part in range(4):
            rows = value_ref[part * 128 : (part + 1) * 128, pl.ds(at, 128)]
            kv_out[BLOCK + part * 128 : BLOCK + (part + 1) * 128] = (
                rows.astype(jnp.float32).T.astype(jnp.bfloat16)
            )


def keys_of(block):
    return block[:BLOCK]


def values_of(block):
    flipped = [block[BLOCK + part * 128 : BLOCK + (part + 1) * 128] for part in range(4)]
    ones = jnp.ones((EXT - HEAD_DIM, BLOCK), jnp.bfloat16)
    return jnp.concatenate([jnp.concatenate(flipped, axis=1), ones], axis=0)


def attend_kernel(place, q_ref, kv_ref, out_ref, best, acc):
    half, y, z = place[0], place[1], place[2]

    def scores(queries, keys):
        return lax.dot_general(keys, queries, CONTRACT_LAST, preferred_element_type=jnp.float32)

    def update(score, values):
        old = best[...]
        new = jnp.maximum(old, jnp.max(score, axis=0, keepdims=True))
        weights = jnp.exp2(score * SCALE - new * SCALE)
        rescale = jnp.exp2((old - new) * SCALE)
        best[...] = new
        acc[...] = acc[...] * rescale + jnp.dot(
            values, weights.astype(jnp.bfloat16), preferred_element_type=jnp.float32
        )

    def one_query_block(slot, _):
        q_half = jnp.where(slot < 4, half, 1 - half)
        q_row = 4 * q_half + lax.rem(y - lax.rem(slot, 4) + 4, 4)
        best[...] = jnp.full_like(best, LOWEST)
        acc[...] = jnp.zeros_like(acc)
        for which in range(2):
            own_row = 4 * half + y
            kv_row = own_row if which == 0 else 7 - own_row

            @pl.when(kv_row < q_row)
            def _():
                tiles = []
                for pair in range(2):
                    blocks = [kv_ref[4 * which + 2 * pair + part] for part in range(2)]
                    keys = jnp.concatenate([keys_of(b) for b in blocks], axis=0)
                    values = jnp.concatenate([values_of(b) for b in blocks], axis=1)
                    tiles.append((scores(q_ref[slot], keys), values))
                for score, values in tiles:
                    update(score, values)

            @pl.when(kv_row == q_row)
            def _():
                block = kv_ref[4 * which]
                score = scores(q_ref[slot], keys_of(block))
                key_at = lax.broadcasted_iota(jnp.int32, (BLOCK, ROWS), 0)
                token = lax.broadcasted_iota(jnp.int32, (BLOCK, ROWS), 1) & (BLOCK - 1)
                update(jnp.where(key_at <= token, score, LOWEST), values_of(block))
                for step in range(1, 4):

                    @pl.when(step <= z)
                    def _():
                        earlier = kv_ref[4 * which + step]
                        update(scores(q_ref[slot], keys_of(earlier)), values_of(earlier))

        total = acc[HEAD_DIM : HEAD_DIM + 1]
        empty = total == 0.0
        inverse = 1.0 / jnp.where(empty, 1.0, total)
        out_ref[slot, :HEAD_DIM] = (acc[:HEAD_DIM] * inverse).astype(jnp.bfloat16)
        level = best[...] * SCALE + jnp.log2(jnp.where(empty, 1.0, total))
        first = level.astype(jnp.bfloat16)
        rest = level - first.astype(jnp.float32)
        second = rest.astype(jnp.bfloat16)
        third = (rest - second.astype(jnp.float32)).astype(jnp.bfloat16)
        index = lax.broadcasted_iota(jnp.int32, (EXT - HEAD_DIM, ROWS), 0)
        rows = jnp.where(
            index == 0,
            first.astype(jnp.float32),
            jnp.where(index == 1, second.astype(jnp.float32), third.astype(jnp.float32)),
        )
        out_ref[slot, HEAD_DIM:] = rows.astype(jnp.bfloat16)
        return 0

    lax.fori_loop(0, 8, one_query_block, 0)


def merge_kernel(place, *refs):
    parts, out_ref = refs[:8], refs[8]
    half = place[0]
    for side in range(2):
        head = half if side == 0 else 1 - half
        group = parts[4 * side : 4 * side + 4]
        levels = []
        for part in group:
            tail = part[HEAD_DIM:].astype(jnp.float32)
            levels.append(tail[0:1] + tail[1:2] + tail[2:3])
        top = jnp.maximum(jnp.maximum(levels[0], levels[1]), jnp.maximum(levels[2], levels[3]))
        shares = [jnp.exp2(level - top) for level in levels]
        inverse = 1.0 / (shares[0] + shares[1] + shares[2] + shares[3])
        mixed = sum(
            part[:HEAD_DIM].astype(jnp.float32) * (share * inverse)
            for part, share in zip(group, shares)
        )
        for sub in range(2):
            at = pl.multiple_of(head * 256 + sub * 128, 128)
            out_ref[:, pl.ds(at, 128)] = mixed[:, sub * BLOCK : (sub + 1) * BLOCK].T.astype(
                jnp.bfloat16
            )


def ring(value, axis, steps):
    size = lax.axis_size(axis)
    return lax.ppermute(value, axis, [(at, (at + steps) % size) for at in range(size)])


def routed(value, target):
    pairs = []
    for half in range(2):
        for y in range(4):
            to_half, to_y = target(half, y)
            pairs.append((4 * half + y, 4 * to_half + to_y))
    return lax.ppermute(value, ("xl", "y"), pairs)


def on_device(query_rows, key_rows, value_rows):
    half, y, z = lax.axis_index("xl"), lax.axis_index("y"), lax.axis_index("z")
    place = jnp.stack([half, y, z]).astype(jnp.int32)
    message = jax.ShapeDtypeStruct((ROWS, 128), jnp.bfloat16)
    q_own, q_other, kv_own, kv_other = pl.pallas_call(
        pack_kernel,
        out_shape=(message,) * 4,
        in_specs=[smem()] + vmem(3),
        out_specs=tuple(vmem(4)),
        compiler_params=PARAMS,
    )(place, query_rows, key_rows, value_rows)
    kv_mirror = routed(kv_other, lambda h, r: (1 - h, 3 - r))
    q_swap = ring(q_other, "xl", 1)
    kv_all = jnp.stack(
        [kv_own] + [ring(kv_own, "z", k) for k in (1, 2, 3)]
        + [kv_mirror] + [ring(kv_mirror, "z", k) for k in (1, 2, 3)]
    )
    q_all = jnp.stack(
        [q_own] + [ring(q_own, "y", k) for k in (1, 2, 3)]
        + [q_swap] + [ring(q_swap, "y", k) for k in (1, 2, 3)]
    )
    partial = pl.pallas_call(
        attend_kernel,
        out_shape=jax.ShapeDtypeStruct((8, EXT, ROWS), jnp.bfloat16),
        in_specs=[smem()] + vmem(2),
        out_specs=vmem(1)[0],
        scratch_shapes=[pltpu.VMEM((1, ROWS), jnp.float32), pltpu.VMEM((EXT, ROWS), jnp.float32)],
        compiler_params=PARAMS,
    )(place, q_all, kv_all)
    parts = [partial[0]]
    parts += [ring(partial[k], "y", 4 - k) for k in (1, 2, 3)]
    parts += [
        routed(partial[4 + k], lambda h, r, k=k: (1 - h, (r - k) % 4)) for k in (0, 1, 2, 3)
    ]
    merged = pl.pallas_call(
        merge_kernel,
        out_shape=jax.ShapeDtypeStruct((BLOCK, 512), jnp.bfloat16),
        in_specs=[smem()] + vmem(8),
        out_specs=vmem(1)[0],
        compiler_params=PARAMS,
    )(place, *parts)
    return lax.all_to_all(merged, ("xh", "core"), split_axis=0, concat_axis=1, tiled=True)


def solution(mesh):
    fine = Mesh(mesh.devices.reshape(2, 4, 4, 2, 2), ("xl", "y", "z", "xh", "core"))
    tokens, heads = ("xl", "y", "z"), ("xh", "core")
    return jax.shard_map(
        on_device,
        mesh=fine,
        in_specs=(P(tokens, heads),) * 3,
        out_specs=P(tokens + heads, None),
        check_vma=False,
    )
```

time: 800 us -> 134 us (0.17)
  local copies, waits for them, and re-layouts: 246 us -> 7.11 us
  matrix products: 138 us -> 0 us
  starting transfers between devices: 187 us -> 50.4 us
  loops' own time: 83.2 us -> 0 us
  other arithmetic: 67.3 us -> 0.08 us
  Pallas kernels: 0 us -> 30.2 us
  waiting for transfers between devices: 36.9 us -> 24.9 us
  blocking collectives: 32.1 us -> 21.3 us
    dot_general x66 -> x0, matrix products: 138 us -> none  [the longest x33 90.1 us: compute(): jnp.einsum('hgqk,khd->hgqd', weights.astype(jnp.bfloat16), v_heads, prefe...]
    ppermute x72 -> x21, starting transfers between devices: 187 us -> 50.4 us  [the longest x16 27.7 us: ring(): lax.ppermute(value, axis, [(at, (at + steps) % size) for at in range(size)])]
    slice x97 -> x0, local copies, waits for them, and re-layouts: 103 us -> none  [the longest x64 85 us: attend_half(): query_pos[-1]]
    reshape x99 -> x0, local copies, waits for them, and re-layouts: 91.2 us -> none  [the longest x33 33.4 us: compute(): v_heads = v_part.reshape(k_count, kv_heads, HEAD_DIM)]
    another operation x65 -> x0, loops' own time: 83.2 us -> none  [the longest x1 80.4 us: on_device(): lax.fori_loop(0, cycle_size - 1, advance, (key_rows, value_rows, states))]
    while x124 -> x0, local copies, waits for them, and re-layouts: 44.1 us -> none
    pallas_call x0 -> x3, Pallas kernels: none -> 30.2 us  [the longest x1 26.4 us: on_device(): pl.pallas_call(attend_kernel, out_shape=jax.ShapeDtypeStruct((8, EXT, ROW...]
    le x33 -> x0, other arithmetic: 27.1 us -> none  [compute(): causal = key_pos[None, :] <= query_pos[:, None]]
  transfers between devices with their start and end apart: 72 -> 21, of which waited for: 10 -> 9; matrix products, arithmetic and copies ran while one was open for 52% -> 0% of each run, Pallas kernels for 0% -> 0%
where the time goes in v1:
time: 134 us
  starting transfers between devices  50.4 us (38%)
  Pallas kernels  30.2 us (23%)
  waiting for transfers between devices  24.9 us (19%)
  blocking collectives  21.3 us (16%)
  local copies, waits for them, and re-layouts  7.11 us (5%)
    ppermute x16, starting transfers between devices, ring(): lax.ppermute(value, axis, [(at, (at + steps) % size) for at in range(size)])  27.7 us
    pallas_call x1, Pallas kernels, on_device(): pl.pallas_call(attend_kernel, out_shape=jax.ShapeDtypeStruct((8, EXT, ROW...  26.4 us
    ppermute x5, starting transfers between devices, routed(): return lax.ppermute(value, ('xl', 'y'), pairs)  22.7 us
    all_to_all x1, blocking collectives, on_device(): lax.all_to_all(merged, ('xh', 'core'), split_axis=0, concat_axis=1, tiled...  21.3 us
    ppermute x16, waiting for transfers between devices, ring(): lax.ppermute(value, axis, [(at, (at + steps) % size) for at in range(size)])  15.6 us
    ppermute x5, waiting for transfers between devices, routed(): return lax.ppermute(value, ('xl', 'y'), pairs)  9.24 us
    unnamed x25, local copies, waits for them, and re-layouts  4.41 us
  transfers between devices with their start and end apart: 21, of which 9 were waited for; matrix products, arithmetic and copies ran while one was open for 0% of the time, Pallas kernels for 0%

profile of v1, /device:TPU:1, one launch (start us, length us, event | category | flops | bytes accessed | tf_op | source)
XLA Modules:
  0.0 134.1 jit_solution(14287053833080250310)
XLA Ops:
  0.1 0.9 copy-done
  1.0 0.9 copy-done.1
  2.0 1.3 shard_map.37
  3.3 2.5 %collective-permute-start.7 = (bf16[1024,128]{1,0:T(8,128)(2,1)S(1)}, bf16[1024,128]{1,0:T(8,128)(2,1)S(1)}, u32[]{:S(2)}, u32[]{:S(2)}) collective-permute-start(bf16[1024,128]{1,0:T(8,128)(2,1)S(1)} %get-tuple-element.11), channel_id=1, source_target_pairs={{0,4},{4,8},{8,12},{12,0},{1,5},{5,9},{9,13},{13,1},{2,6},{6,10},{... | collective-permute-start | bytes 786440 | tf_op jit(solution)/shard_map/ppermute | solution.py:150
  5.8 3.3 %collective-permute-start.8 = (bf16[1024,128]{1,0:T(8,128)(2,1)S(1)}, bf16[1024,128]{1,0:T(8,128)(2,1)S(1)}, u32[]{:S(2)}, u32[]{:S(2)}) collective-permute-start(bf16[1024,128]{1,0:T(8,128)(2,1)S(1)} %get-tuple-element.11), channel_id=1, source_target_pairs={{0,8},{4,12},{8,0},{12,4},{1,9},{5,13},{9,1},{13,5},{2,10},{6,14},... | collective-permute-start | bytes 786440 | tf_op jit(solution)/shard_map/ppermute | solution.py:150
  9.9 1.3 collective-permute-start
  11.1 2.6 %collective-permute-start.1 = (bf16[1024,128]{1,0:T(8,128)(2,1)S(1)}, bf16[1024,128]{1,0:T(8,128)(2,1)S(1)}, u32[]{:S(2)}, u32[]{:S(2)}) collective-permute-start(bf16[1024,128]{1,0:T(8,128)(2,1)S(1)} %get-tuple-element.9), channel_id=1, source_target_pairs={{0,32},{16,48},{32,0},{48,16},{1,33},{17,49},{33,1},{49,17},{2,34}... | collective-permute-start | bytes 786440 | tf_op jit(solution)/shard_map/ppermute | solution.py:150
  14.0 3.7 %collective-permute-start.10 = (bf16[1024,128]{1,0:T(8,128)(2,1)S(1)}, bf16[1024,128]{1,0:T(8,128)(2,1)S(1)}, u32[]{:S(2)}, u32[]{:S(2)}) collective-permute-start(bf16[1024,128]{1,0:T(8,128)(2,1)S(1)} %get-tuple-element.12), channel_id=1, source_target_pairs={{0,112},{16,96},{32,80},{48,64},{64,48},{80,32},{96,16},{112,0},{1... | collective-permute-start | bytes 786440 | tf_op jit(solution)/shard_map/ppermute | solution.py:159
  17.7 2.8 %collective-permute-done.8 = bf16[1024,128]{1,0:T(8,128)(2,1)S(1)} collective-permute-done((bf16[1024,128]{1,0:T(8,128)(2,1)S(1)}, bf16[1024,128]{1,0:T(8,128)(2,1)S(1)}, u32[]{:S(2)}, u32[]{:S(2)}) %collective-permute-start.8) | collective-permute-done | bytes 262176 | tf_op jit(solution)/shard_map/ppermute | solution.py:150
  20.4 2.7 %collective-permute-start.2 = (bf16[1024,128]{1,0:T(8,128)(2,1)S(1)}, bf16[1024,128]{1,0:T(8,128)(2,1)S(1)}, u32[]{:S(2)}, u32[]{:S(2)}) collective-permute-start(bf16[1024,128]{1,0:T(8,128)(2,1)S(1)} %get-tuple-element.9), channel_id=1, source_target_pairs={{0,48},{16,0},{32,16},{48,32},{1,49},{17,1},{33,17},{49,33},{2,50}... | collective-permute-start | bytes 786440 | tf_op jit(solution)/shard_map/ppermute | solution.py:150
  23.2 1.3 collective-permute-start.3
  25.4 1.5 %collective-permute-start.12 = (bf16[1024,128]{1,0:T(8,128)(2,1)S(1)}, bf16[1024,128]{1,0:T(8,128)(2,1)S(1)}, u32[]{:S(2)}, u32[]{:S(2)}) collective-permute-start(bf16[1024,128]{1,0:T(8,128)(2,1)S(1)} %collective-permute-done.10), channel_id=1, source_target_pairs={{0,8},{4,12},{8,0},{12,4},{1,9},{5,13},{9,1},{13,5},{2,10},{6,14},... | collective-permute-start | bytes 786440 | tf_op jit(solution)/shard_map/ppermute | solution.py:150
  27.0 1.3 collective-permute-start.13
  28.3 1.0 collective-permute-done.3
  29.3 2.2 %collective-permute-start.4 = (bf16[1024,128]{1,0:T(8,128)(2,1)S(1)}, bf16[1024,128]{1,0:T(8,128)(2,1)S(1)}, u32[]{:S(2)}, u32[]{:S(2)}) collective-permute-start(bf16[1024,128]{1,0:T(8,128)(2,1)S(1)} %collective-permute-done.3), channel_id=1, source_target_pairs={{0,16},{16,32},{32,48},{48,0},{1,17},{17,33},{33,49},{49,1},{2,18}... | collective-permute-start | bytes 786440 | tf_op jit(solution)/shard_map/ppermute | solution.py:150
  31.5 2.1 %collective-permute-start.5 = (bf16[1024,128]{1,0:T(8,128)(2,1)S(1)}, bf16[1024,128]{1,0:T(8,128)(2,1)S(1)}, u32[]{:S(2)}, u32[]{:S(2)}) collective-permute-start(bf16[1024,128]{1,0:T(8,128)(2,1)S(1)} %collective-permute-done.3), channel_id=1, source_target_pairs={{0,32},{16,48},{32,0},{48,16},{1,33},{17,49},{33,1},{49,17},{2,34}... | collective-permute-start | bytes 786440 | tf_op jit(solution)/shard_map/ppermute | solution.py:150
  33.7 1.6 %collective-permute-done.11 = bf16[1024,128]{1,0:T(8,128)(2,1)S(1)} collective-permute-done((bf16[1024,128]{1,0:T(8,128)(2,1)S(1)}, bf16[1024,128]{1,0:T(8,128)(2,1)S(1)}, u32[]{:S(2)}, u32[]{:S(2)}) %collective-permute-start.11) | collective-permute-done | bytes 262176 | tf_op jit(solution)/shard_map/ppermute | solution.py:150
  35.3 1.3 %collective-permute-start.6 = (bf16[1024,128]{1,0:T(8,128)(2,1)S(1)}, bf16[1024,128]{1,0:T(8,128)(2,1)S(1)}, u32[]{:S(2)}, u32[]{:S(2)}) collective-permute-start(bf16[1024,128]{1,0:T(8,128)(2,1)S(1)} %collective-permute-done.3), channel_id=1, source_target_pairs={{0,48},{16,0},{32,16},{48,32},{1,49},{17,1},{33,17},{49,33},{2,50}... | collective-permute-start | bytes 786440 | tf_op jit(solution)/shard_map/ppermute | solution.py:150
  36.9 3.5 %collective-permute-done.5 = bf16[1024,128]{1,0:T(8,128)(2,1)S(1)} collective-permute-done((bf16[1024,128]{1,0:T(8,128)(2,1)S(1)}, bf16[1024,128]{1,0:T(8,128)(2,1)S(1)}, u32[]{:S(2)}, u32[]{:S(2)}) %collective-permute-start.5) | collective-permute-done | bytes 262176 | tf_op jit(solution)/shard_map/ppermute | solution.py:150
  40.4 6.6 %collective-permute-done.6 = bf16[1024,128]{1,0:T(8,128)(2,1)S(1)} collective-permute-done((bf16[1024,128]{1,0:T(8,128)(2,1)S(1)}, bf16[1024,128]{1,0:T(8,128)(2,1)S(1)}, u32[]{:S(2)}, u32[]{:S(2)}) %collective-permute-start.6) | collective-permute-done | bytes 262176 | tf_op jit(solution)/shard_map/ppermute | solution.py:150
  47.0 1.3 copy-done.2
  48.3 26.4 %shard_map.38 = bf16[8,144,1024]{2,1,0:T(8,128)(2,1)} custom-call(s32[3]{0:T(128)S(1)} %pad_add_fusion.place, bf16[8,1024,128]{2,1,0:T(8,128)(2,1)} %copy-done.2, bf16[8,1024,128]{2,1,0:T(8,128)(2,1)} %copy-done.3), custom_call_target="tpu_custom_call" | custom-call | tf_op jit(solution)/shard_map/pallas_call | solution.py:183
  74.8 1.8 %slice_bitcast_fusion = (bf16[144,1024]{1,0:T(8,128)(2,1)S(1)}, bf16[144,1024]{1,0:T(8,128)(2,1)S(1)}, bf16[144,1024]{1,0:T(8,128)(2,1)S(1)}, bf16[144,1024]{1,0...) fusion(bf16[8,144,1024]{2,1,0:T(8,128)(2,1)} %shard_map.38), kind=kLoop, calls=%fused_computation | loop fusion | bytes 4718592 | tf_op jit(solution)/shard_map/squeeze | solution.py:194
  76.7 4.6 %collective-permute-start.15 = (bf16[144,1024]{1,0:T(8,128)(2,1)S(1)}, bf16[144,1024]{1,0:T(8,128)(2,1)S(1)}, u32[]{:S(2)}, u32[]{:S(2)}) collective-permute-start(bf16[144,1024]{1,0:T(8,128)(2,1)S(1)} %get-tuple-element.18), channel_id=1, source_target_pairs={{0,32},{16,48},{32,0},{48,16},{1,33},{17,49},{33,1},{49,17},{2,34}... | collective-permute-start | bytes 884744 | tf_op jit(solution)/shard_map/ppermute | solution.py:150
  81.3 1.2 collective-permute-start.17
  82.5 2.6 %collective-permute-start.18 = (bf16[144,1024]{1,0:T(8,128)(2,1)S(1)}, bf16[144,1024]{1,0:T(8,128)(2,1)S(1)}, u32[]{:S(2)}, u32[]{:S(2)}) collective-permute-start(bf16[144,1024]{1,0:T(8,128)(2,1)S(1)} %get-tuple-element.15), channel_id=1, source_target_pairs={{0,112},{16,64},{32,80},{48,96},{64,48},{80,0},{96,16},{112,32},{1... | collective-permute-start | bytes 884744 | tf_op jit(solution)/shard_map/ppermute | solution.py:159
  85.2 2.6 %collective-permute-start.19 = (bf16[144,1024]{1,0:T(8,128)(2,1)S(1)}, bf16[144,1024]{1,0:T(8,128)(2,1)S(1)}, u32[]{:S(2)}, u32[]{:S(2)}) collective-permute-start(bf16[144,1024]{1,0:T(8,128)(2,1)S(1)} %get-tuple-element.14), channel_id=1, source_target_pairs={{0,96},{16,112},{32,64},{48,80},{64,32},{80,48},{96,0},{112,16},{1... | collective-permute-start | bytes 884744 | tf_op jit(solution)/shard_map/ppermute | solution.py:159
  87.7 12.6 %collective-permute-start.20 = (bf16[144,1024]{1,0:T(8,128)(2,1)S(1)}, bf16[144,1024]{1,0:T(8,128)(2,1)S(1)}, u32[]{:S(2)}, u32[]{:S(2)}) collective-permute-start(bf16[144,1024]{1,0:T(8,128)(2,1)S(1)} %get-tuple-element.13), channel_id=1, source_target_pairs={{0,80},{16,96},{32,112},{48,64},{64,16},{80,32},{96,48},{112,0},{1... | collective-permute-start | bytes 884744 | tf_op jit(solution)/shard_map/ppermute | solution.py:159
  100.8 8.1 %collective-permute-done.20.refs_7_ = bf16[144,1024]{1,0:T(8,128)(2,1)S(1)} collective-permute-done((bf16[144,1024]{1,0:T(8,128)(2,1)S(1)}, bf16[144,1024]{1,0:T(8,128)(2,1)S(1)}, u32[]{:S(2)}, u32[]{:S(2)}) %collective-permute-start.20) | collective-permute-done | bytes 294944 | tf_op jit(solution)/shard_map/ppermute | solution.py:159
  109.5 2.5 %shard_map.39 = bf16[512,512]{1,0:T(8,128)(2,1)} custom-call(s32[3]{0:T(128)S(1)} %pad_add_fusion.place, bf16[144,1024]{1,0:T(8,128)(2,1)S(1)} %get-tuple-element.20.refs_0_, bf16[144,1024]{1,0:T(8,128)(2,1)S(1)} %collective-permute-done.14.refs_1_, bf16[144,1024]{1,0:T(8,128)(2,1)S(1)} %collective-permute-done.15.refs_2_, ...), custom_call_target="tpu_custom_call" | custom-call | tf_op jit(solution)/shard_map/pallas_call | solution.py:196
  112.0 21.3 %all_to_all.19 = bf16[4,128,512]{2,1,0:T(8,128)(2,1)S(1)} all-to-all(bf16[4,128,512]{2,1,0:T(8,128)(2,1)} %bitcast.56), channel_id=1, replica_groups=mesh['xl'=2,'y'=4,'z'=4,'xh'=2,'core'=2] {'xh','core'}, dimensions={0} | all-to-all | bytes 1048576 | tf_op jit(solution)/shard_map/all_to_all | solution.py:203
  133.3 0.8 copy.5
  (44 shorter events, 3.5 us)
Async XLA Ops:
  0.1 1.0 copy-start
  1.0 0.9 copy-start.1
  3.3 10.7 %collective-permute-start.7 = (bf16[1024,128]{1,0:T(8,128)(2,1)S(1)}, bf16[1024,128]{1,0:T(8,128)(2,1)S(1)}, u32[]{:S(2)}, u32[]{:S(2)}) collective-permute-start(bf16[1024,128]{1,0:T(8,128)(2,1)S(1)} %get-tuple-element.11), channel_id=1, source_target_pairs={{0,4},{4,8},{8,12},{12,0},{1,5},{5,9},{9,13},{13,1},{2,6},{6,10},{... | collective-permute-start | bytes 786440 | tf_op jit(solution)/shard_map/ppermute | solution.py:150
  5.8 14.6 %collective-permute-start.8 = (bf16[1024,128]{1,0:T(8,128)(2,1)S(1)}, bf16[1024,128]{1,0:T(8,128)(2,1)S(1)}, u32[]{:S(2)}, u32[]{:S(2)}) collective-permute-start(bf16[1024,128]{1,0:T(8,128)(2,1)S(1)} %get-tuple-element.11), channel_id=1, source_target_pairs={{0,8},{4,12},{8,0},{12,4},{1,9},{5,13},{9,1},{13,5},{2,10},{6,14},... | collective-permute-start | bytes 786440 | tf_op jit(solution)/shard_map/ppermute | solution.py:150
  9.1 14.1 %collective-permute-start.9 = (bf16[1024,128]{1,0:T(8,128)(2,1)S(1)}, bf16[1024,128]{1,0:T(8,128)(2,1)S(1)}, u32[]{:S(2)}, u32[]{:S(2)}) collective-permute-start(bf16[1024,128]{1,0:T(8,128)(2,1)S(1)} %get-tuple-element.11), channel_id=1, source_target_pairs={{0,12},{4,0},{8,4},{12,8},{1,13},{5,1},{9,5},{13,9},{2,14},{6,2},{... | collective-permute-start | bytes 786440 | tf_op jit(solution)/shard_map/ppermute | solution.py:150
  9.9 15.5 %collective-permute-start = (bf16[1024,128]{1,0:T(8,128)(2,1)S(1)}, bf16[1024,128]{1,0:T(8,128)(2,1)S(1)}, u32[]{:S(2)}, u32[]{:S(2)}) collective-permute-start(bf16[1024,128]{1,0:T(8,128)(2,1)S(1)} %get-tuple-element.9), channel_id=1, source_target_pairs={{0,16},{16,32},{32,48},{48,0},{1,17},{17,33},{33,49},{49,1},{2,18}... | collective-permute-start | bytes 786440 | tf_op jit(solution)/shard_map/ppermute | solution.py:150
  11.1 15.8 %collective-permute-start.1 = (bf16[1024,128]{1,0:T(8,128)(2,1)S(1)}, bf16[1024,128]{1,0:T(8,128)(2,1)S(1)}, u32[]{:S(2)}, u32[]{:S(2)}) collective-permute-start(bf16[1024,128]{1,0:T(8,128)(2,1)S(1)} %get-tuple-element.9), channel_id=1, source_target_pairs={{0,32},{16,48},{32,0},{48,16},{1,33},{17,49},{33,1},{49,17},{2,34}... | collective-permute-start | bytes 786440 | tf_op jit(solution)/shard_map/ppermute | solution.py:150
  14.0 11.3 %collective-permute-start.10 = (bf16[1024,128]{1,0:T(8,128)(2,1)S(1)}, bf16[1024,128]{1,0:T(8,128)(2,1)S(1)}, u32[]{:S(2)}, u32[]{:S(2)}) collective-permute-start(bf16[1024,128]{1,0:T(8,128)(2,1)S(1)} %get-tuple-element.12), channel_id=1, source_target_pairs={{0,112},{16,96},{32,80},{48,64},{64,48},{80,32},{96,16},{112,0},{1... | collective-permute-start | bytes 786440 | tf_op jit(solution)/shard_map/ppermute | solution.py:159
  20.4 11.1 %collective-permute-start.2 = (bf16[1024,128]{1,0:T(8,128)(2,1)S(1)}, bf16[1024,128]{1,0:T(8,128)(2,1)S(1)}, u32[]{:S(2)}, u32[]{:S(2)}) collective-permute-start(bf16[1024,128]{1,0:T(8,128)(2,1)S(1)} %get-tuple-element.9), channel_id=1, source_target_pairs={{0,48},{16,0},{32,16},{48,32},{1,49},{17,1},{33,17},{49,33},{2,50}... | collective-permute-start | bytes 786440 | tf_op jit(solution)/shard_map/ppermute | solution.py:150
  23.2 6.1 %collective-permute-start.3 = (bf16[1024,128]{1,0:T(8,128)(2,1)S(1)}, bf16[1024,128]{1,0:T(8,128)(2,1)S(1)}, u32[]{:S(2)}, u32[]{:S(2)}) collective-permute-start(bf16[1024,128]{1,0:T(8,128)(2,1)S(1)} %get-tuple-element.10), channel_id=1, source_target_pairs={{0,64},{64,0},{1,65},{65,1},{2,66},{66,2},{3,67},{67,3},{4,68},{68... | collective-permute-start | bytes 786440 | tf_op jit(solution)/shard_map/ppermute | solution.py:150
  25.3 10.0 %collective-permute-start.11 = (bf16[1024,128]{1,0:T(8,128)(2,1)S(1)}, bf16[1024,128]{1,0:T(8,128)(2,1)S(1)}, u32[]{:S(2)}, u32[]{:S(2)}) collective-permute-start(bf16[1024,128]{1,0:T(8,128)(2,1)S(1)} %collective-permute-done.10), channel_id=1, source_target_pairs={{0,4},{4,8},{8,12},{12,0},{1,5},{5,9},{9,13},{13,1},{2,6},{6,10},{... | collective-permute-start | bytes 786440 | tf_op jit(solution)/shard_map/ppermute | solution.py:150
  25.4 11.3 %collective-permute-start.12 = (bf16[1024,128]{1,0:T(8,128)(2,1)S(1)}, bf16[1024,128]{1,0:T(8,128)(2,1)S(1)}, u32[]{:S(2)}, u32[]{:S(2)}) collective-permute-start(bf16[1024,128]{1,0:T(8,128)(2,1)S(1)} %collective-permute-done.10), channel_id=1, source_target_pairs={{0,8},{4,12},{8,0},{12,4},{1,9},{5,13},{9,1},{13,5},{2,10},{6,14},... | collective-permute-start | bytes 786440 | tf_op jit(solution)/shard_map/ppermute | solution.py:150
  27.0 9.8 %collective-permute-start.13 = (bf16[1024,128]{1,0:T(8,128)(2,1)S(1)}, bf16[1024,128]{1,0:T(8,128)(2,1)S(1)}, u32[]{:S(2)}, u32[]{:S(2)}) collective-permute-start(bf16[1024,128]{1,0:T(8,128)(2,1)S(1)} %collective-permute-done.10), channel_id=1, source_target_pairs={{0,12},{4,0},{8,4},{12,8},{1,13},{5,1},{9,5},{13,9},{2,14},{6,2},{... | collective-permute-start | bytes 786440 | tf_op jit(solution)/shard_map/ppermute | solution.py:150
  29.3 7.5 %collective-permute-start.4 = (bf16[1024,128]{1,0:T(8,128)(2,1)S(1)}, bf16[1024,128]{1,0:T(8,128)(2,1)S(1)}, u32[]{:S(2)}, u32[]{:S(2)}) collective-permute-start(bf16[1024,128]{1,0:T(8,128)(2,1)S(1)} %collective-permute-done.3), channel_id=1, source_target_pairs={{0,16},{16,32},{32,48},{48,0},{1,17},{17,33},{33,49},{49,1},{2,18}... | collective-permute-start | bytes 786440 | tf_op jit(solution)/shard_map/ppermute | solution.py:150
  31.5 8.8 %collective-permute-start.5 = (bf16[1024,128]{1,0:T(8,128)(2,1)S(1)}, bf16[1024,128]{1,0:T(8,128)(2,1)S(1)}, u32[]{:S(2)}, u32[]{:S(2)}) collective-permute-start(bf16[1024,128]{1,0:T(8,128)(2,1)S(1)} %collective-permute-done.3), channel_id=1, source_target_pairs={{0,32},{16,48},{32,0},{48,16},{1,33},{17,49},{33,1},{49,17},{2,34}... | collective-permute-start | bytes 786440 | tf_op jit(solution)/shard_map/ppermute | solution.py:150
  35.3 11.6 %collective-permute-start.6 = (bf16[1024,128]{1,0:T(8,128)(2,1)S(1)}, bf16[1024,128]{1,0:T(8,128)(2,1)S(1)}, u32[]{:S(2)}, u32[]{:S(2)}) collective-permute-start(bf16[1024,128]{1,0:T(8,128)(2,1)S(1)} %collective-permute-done.3), channel_id=1, source_target_pairs={{0,48},{16,0},{32,16},{48,32},{1,49},{17,1},{33,17},{49,33},{2,50}... | collective-permute-start | bytes 786440 | tf_op jit(solution)/shard_map/ppermute | solution.py:150
  36.8 10.2 %copy-start.3 = (bf16[8,1024,128]{2,1,0:T(8,128)(2,1)}, bf16[8,1024,128]{2,1,0:T(8,128)(2,1)S(1)}, u32[]{:S(2)}) copy-start(bf16[8,1024,128]{2,1,0:T(8,128)(2,1)S(1)} %bitcast_dynamic-update-slice_fusion.kv_ref) | copy-start | bytes 6291460
  47.0 1.3 copy-start.2
  76.6 8.6 %collective-permute-start.14 = (bf16[144,1024]{1,0:T(8,128)(2,1)S(1)}, bf16[144,1024]{1,0:T(8,128)(2,1)S(1)}, u32[]{:S(2)}, u32[]{:S(2)}) collective-permute-start(bf16[144,1024]{1,0:T(8,128)(2,1)S(1)} %get-tuple-element.19), channel_id=1, source_target_pairs={{0,48},{16,0},{32,16},{48,32},{1,49},{17,1},{33,17},{49,33},{2,50}... | collective-permute-start | bytes 884744 | tf_op jit(solution)/shard_map/ppermute | solution.py:150
  76.7 11.1 %collective-permute-start.15 = (bf16[144,1024]{1,0:T(8,128)(2,1)S(1)}, bf16[144,1024]{1,0:T(8,128)(2,1)S(1)}, u32[]{:S(2)}, u32[]{:S(2)}) collective-permute-start(bf16[144,1024]{1,0:T(8,128)(2,1)S(1)} %get-tuple-element.18), channel_id=1, source_target_pairs={{0,32},{16,48},{32,0},{48,16},{1,33},{17,49},{33,1},{49,17},{2,34}... | collective-permute-start | bytes 884744 | tf_op jit(solution)/shard_map/ppermute | solution.py:150
  81.3 19.1 %collective-permute-start.16 = (bf16[144,1024]{1,0:T(8,128)(2,1)S(1)}, bf16[144,1024]{1,0:T(8,128)(2,1)S(1)}, u32[]{:S(2)}, u32[]{:S(2)}) collective-permute-start(bf16[144,1024]{1,0:T(8,128)(2,1)S(1)} %get-tuple-element.17), channel_id=1, source_target_pairs={{0,16},{16,32},{32,48},{48,0},{1,17},{17,33},{33,49},{49,1},{2,18}... | collective-permute-start | bytes 884744 | tf_op jit(solution)/shard_map/ppermute | solution.py:150
  81.3 19.1 %collective-permute-start.17 = (bf16[144,1024]{1,0:T(8,128)(2,1)S(1)}, bf16[144,1024]{1,0:T(8,128)(2,1)S(1)}, u32[]{:S(2)}, u32[]{:S(2)}) collective-permute-start(bf16[144,1024]{1,0:T(8,128)(2,1)S(1)} %get-tuple-element.16), channel_id=1, source_target_pairs={{0,64},{16,80},{32,96},{48,112},{64,0},{80,16},{96,32},{112,48},{1... | collective-permute-start | bytes 884744 | tf_op jit(solution)/shard_map/ppermute | solution.py:159
  82.5 17.8 %collective-permute-start.18 = (bf16[144,1024]{1,0:T(8,128)(2,1)S(1)}, bf16[144,1024]{1,0:T(8,128)(2,1)S(1)}, u32[]{:S(2)}, u32[]{:S(2)}) collective-permute-start(bf16[144,1024]{1,0:T(8,128)(2,1)S(1)} %get-tuple-element.15), channel_id=1, source_target_pairs={{0,112},{16,64},{32,80},{48,96},{64,48},{80,0},{96,16},{112,32},{1... | collective-permute-start | bytes 884744 | tf_op jit(solution)/shard_map/ppermute | solution.py:159
  85.2 15.6 %collective-permute-start.19 = (bf16[144,1024]{1,0:T(8,128)(2,1)S(1)}, bf16[144,1024]{1,0:T(8,128)(2,1)S(1)}, u32[]{:S(2)}, u32[]{:S(2)}) collective-permute-start(bf16[144,1024]{1,0:T(8,128)(2,1)S(1)} %get-tuple-element.14), channel_id=1, source_target_pairs={{0,96},{16,112},{32,64},{48,80},{64,32},{80,48},{96,0},{112,16},{1... | collective-permute-start | bytes 884744 | tf_op jit(solution)/shard_map/ppermute | solution.py:159
  87.7 21.1 %collective-permute-start.20 = (bf16[144,1024]{1,0:T(8,128)(2,1)S(1)}, bf16[144,1024]{1,0:T(8,128)(2,1)S(1)}, u32[]{:S(2)}, u32[]{:S(2)}) collective-permute-start(bf16[144,1024]{1,0:T(8,128)(2,1)S(1)} %get-tuple-element.13), channel_id=1, source_target_pairs={{0,80},{16,96},{32,112},{48,64},{64,16},{80,32},{96,48},{112,0},{1... | collective-permute-start | bytes 884744 | tf_op jit(solution)/shard_map/ppermute | solution.py:159
  100.8 8.1 %copy-start.4 = (bf16[144,1024]{1,0:T(8,128)(2,1)}, bf16[144,1024]{1,0:T(8,128)(2,1)S(1)}, u32[]{:S(2)}) copy-start(bf16[144,1024]{1,0:T(8,128)(2,1)S(1)} %collective-permute-done.19.refs_6_) | copy-start | bytes 884740
  108.8 0.7 copy-start.5
